TPU v7x, 32 devices: a whole 2x2x4 slice. The times are simulated.
32 devices in a mesh: lists: 4 (over x, core), score: 8 (over z, y).
Axes of the slice: x: 2, y: 2, z: 4, core: 2. Of those that a mesh axis runs over, the one named last changes fastest.
Arguments:
- queries: bfloat16 [256, 32, 128], P('score', 'lists'), may hold values from -0.59765625 to 0.59765625
- centroids: bfloat16 [32768, 128], P('lists'), may hold values from -3 to 3
- codes: bfloat16 [1024, 128, 128], P(('lists', 'score')), may hold values from -6 to 6
- scales: float32 [1024, 128], P(('lists', 'score')), may hold values from 0.1 to 1
- centroid_ids: int32 [1024, 128], P(('lists', 'score')), may hold values from 0 to 8191
- lengths: int32 [1024], P(('lists', 'score')), may hold values from 1 to 128
- owners: int32 [4, 256, 8], P('lists', 'score'), may hold values from 0 to 31, all different within a row; in each aligned block of 32 rows (0 to 31, 32 to 63, ..., all dimensions but the last counted through in order) at most 16 rows name the same one
- slots: int32 [4, 256, 8], P('lists', 'score'), may hold values from 0 to 31
Outputs:
- scores: float32 [4, 256, 8], P('lists', 'score')
- relevance: float32 [256, 32768], P('score', 'lists')
Inputs may be any that keep to these rules, and one draw needn't show every extreme that they name: Within the 32 rows of one device (aligned blocks of 32 rows, the first two dimensions taken together in order) no owner is named more than 16 times; each row names 8 different owners. Owner d holds blocks d * 32 to d * 32 + 31. `centroid_ids`: A row among the 8192 centroids of the block's lists shard.
All inputs are finite; a program needn't handle non-finite values.
Results may differ from a plain program's by a relative error of at most 0.00034.
Values may be sent and summed in bfloat16 or wider, within the bound.
A program may use at most 128 MiB of HBM per device.

v0:
```python
import math

import jax
import jax.numpy as jnp
from jax import lax
from jax.sharding import PartitionSpec as P


def rebuild_held(codes, scales, centroid_ids, centroids):
    held = codes.shape[0]
    slot_len = codes.shape[1]
    width = codes.shape[2]
    base = (
        jnp.take(centroids, centroid_ids.reshape(-1), axis=0)
        .astype(jnp.float32)
        .reshape(held, slot_len, width)
    )
    vectors = base + scales[..., None] * codes.astype(jnp.float32)
    return vectors.astype(jnp.bfloat16).reshape(held, slot_len * width)


def pick_blocks(held_vectors, lengths, wanted):
    held = held_vectors.shape[0]
    picker = wanted[:, None] == jnp.arange(held, dtype=jnp.int32)[None, :]
    picked = jnp.dot(
        picker.astype(jnp.bfloat16), held_vectors, preferred_element_type=jnp.float32
    ).astype(jnp.bfloat16)
    picked_len = jnp.sum(jnp.where(picker, lengths[None, :], 0), axis=1)
    return (picked, picked_len)


def maxsim_total(inner, valid_count, token_count):
    spots = jnp.arange(inner.shape[-1], dtype=jnp.int32)
    keep = spots < valid_count[..., None, None]
    best = jnp.max(jnp.where(keep, inner, -1e30), axis=-1)
    return jnp.sum(best, axis=-1) / token_count


def per_device(queries, centroids, codes, scales, centroid_ids, lengths, owners, slots):
    gathered = lax.all_gather(queries, "lists", axis=1, tiled=True)
    query_rows, token_count, width = gathered.shape
    slot_len = codes.shape[1]
    cent_rows = centroids.shape[0]
    group = math.gcd(cent_rows, 4096)
    flat = gathered.reshape(query_rows * token_count, width)
    grouped = centroids.reshape(cent_rows // group, group, width)

    def relate(block_rows):
        inner = lax.dot_general(
            flat, block_rows, (((1,), (1,)), ((), ())), preferred_element_type=jnp.float32
        )
        return jnp.max(inner.reshape(query_rows, token_count, group), axis=1)

    relevance = jnp.transpose(lax.map(relate, grouped), (1, 0, 2)).reshape(query_rows, cent_rows)
    held_vectors = rebuild_held(codes, scales, centroid_ids, centroids)
    owner_flat = owners[0].reshape(-1)
    local_flat = slots[0].reshape(-1)
    count = owner_flat.shape[0]
    per_query = owners.shape[2]
    devices = lax.axis_size("lists") * lax.axis_size("score")
    capacity = max(4, 2 * -(-count // devices))
    total_slots = devices * capacity
    matches = (owner_flat[:, None] == jnp.arange(devices, dtype=jnp.int32)[None, :]).astype(
        jnp.float32
    )
    positions = jnp.arange(count, dtype=jnp.int32)
    before = (positions[:, None] > positions[None, :]).astype(jnp.float32)
    prior = jnp.dot(
        before, matches, precision=lax.Precision.HIGHEST, preferred_element_type=jnp.float32
    )
    earlier = jnp.sum(prior * matches, axis=1).astype(jnp.int32)
    placed = owner_flat * capacity + earlier
    slot_match = placed[None, :] == jnp.arange(total_slots, dtype=jnp.int32)[:, None]
    request = jnp.sum(jnp.where(slot_match, local_flat[None, :], 0), axis=1).reshape(
        devices, capacity
    )
    slot_pick = slot_match.astype(jnp.bfloat16)
    row_pick = (
        (positions // per_query)[:, None] == jnp.arange(query_rows, dtype=jnp.int32)[None, :]
    ).astype(jnp.bfloat16)
    selector = jnp.dot(slot_pick, row_pick, preferred_element_type=jnp.float32).astype(jnp.bfloat16)
    outgoing = jnp.dot(
        selector,
        gathered.reshape(query_rows, token_count * width),
        preferred_element_type=jnp.float32,
    )
    outgoing = outgoing.astype(jnp.bfloat16).reshape(devices, capacity, token_count, width)
    wanted = lax.all_to_all(request, ("lists", "score"), split_axis=0, concat_axis=0, tiled=True)
    asked = lax.all_to_all(outgoing, ("lists", "score"), split_axis=0, concat_axis=0, tiled=True)
    vectors, valid = pick_blocks(held_vectors, lengths, wanted.reshape(-1))
    vectors = vectors.reshape(wanted.shape + (slot_len, width))
    valid = valid.reshape(wanted.shape)
    inner = jnp.einsum("sctd,scpd->sctp", asked, vectors, preferred_element_type=jnp.float32)
    returned = lax.all_to_all(
        maxsim_total(inner, valid, token_count),
        ("lists", "score"),
        split_axis=0,
        concat_axis=0,
        tiled=True,
    )
    scores = returned.reshape(-1)[placed].reshape(query_rows, per_query)
    return (scores[None], relevance)


def solution(mesh):
    placed = (
        P("score", "lists", None),
        P("lists", None),
        P(("lists", "score"), None, None),
        P(("lists", "score"), None),
        P(("lists", "score"), None),
        P(("lists", "score")),
        P("lists", "score", None),
        P("lists", "score", None),
    )
    return jax.shard_map(
        per_device,
        mesh=mesh,
        in_specs=placed,
        out_specs=(P("lists", "score", None), P("score", "lists")),
        check_vma=False,
    )
```

profile of v0, /device:TPU:0, one launch (start us, length us, event | category | flops | bytes accessed | tf_op | source)
XLA Modules:
  0.0 154.9 jit_solution(18240172773380530800)
XLA Ops:
  0.6 0.8 copy.22
  1.7 0.8 copy.23
  2.7 0.7 all_to_all.13
  3.4 7.3 %all-to-all-start = ((s32[32,1,16]{2,1,0:T(1,128)}), s32[32,1,16]{2,1,0:T(1,128)S(1)}, u32[]{:S(2)}, u32[]{:S(2)}) async-start(s32[32,1,16]{2,1,0:T(1,128)} %bitcast.4), calls=%async_computation | async-start | bytes 32768 | tf_op jit(solution)/shard_map/all_to_all | solution.py:88
  10.7 6.3 %all_gather.3 = bf16[32,32,128]{2,1,0:T(8,128)(2,1)S(1)} all-gather(bf16[32,8,128]{2,1,0:T(8,128)(2,1)} %param.10), channel_id=1, replica_groups=mesh['lists'=4,'score'=8] {'lists'}, dimensions={1}, use_global_device_ids=true | all-gather | bytes 327680 | tf_op jit(solution)/shard_map/all_gather | solution.py:40
  17.1 3.5 %fusion.9 = bf16[64,8,32,128]{3,1,2,0:T(8,128)(2,1)} fusion(bf16[4,8,32,128]{3,2,1,0:T(8,128)(2,1)S(1)} %bitcast.62, s32[256]{0:T(256)S(1)} %get-tuple-element.40, s32[256]{0:T(256)S(1)} %get-tuple-element.39), kind=kOutput, calls=%fused_computation.14 | convolution fusion | flops 144859136 | bytes 4458496 | tf_op jit(solution)/shard_map/dot_general | solution.py:82
  20.5 5.4 %copy.31 = bf16[64,8,32,128]{3,2,1,0:T(8,128)(2,1)} copy(bf16[64,8,32,128]{3,1,2,0:T(8,128)(2,1)} %fusion.9) | data formatting | bytes 8388608
  25.9 5.8 %all-to-all-start.1 = ((bf16[32,16,32,128]{3,2,1,0:T(8,128)(2,1)}), bf16[32,16,32,128]{3,2,1,0:T(8,128)(2,1)}, u32[]{:S(2)}, u32[]{:S(2)}) async-start(bf16[32,16,32,128]{3,2,1,0:T(8,128)(2,1)} %bitcast.59), calls=%async_computation.1 | async-start | bytes 8388608 | tf_op jit(solution)/shard_map/all_to_all | solution.py:89
  32.1 15.0 %gather_fusion = bf16[4096,128]{1,0:T(8,128)(2,1)} fusion(bf16[8192,128]{1,0:T(8,128)(2,1)S(1)} %copy-done, s32[4096]{0:T(1024)S(1)} %broadcast_clamp_fusion), kind=kCustom, calls=%fused_computation | custom fusion | bytes 2113536 | tf_op jit(solution)/shard_map/jit(_take)/gather | solution.py:14
  47.1 3.2 %add_convert_fusion = bf16[32,128,128]{2,1,0:T(8,128)(2,1)S(1)} fusion(bf16[32,128,128]{2,1,0:T(8,128)(2,1)} %param.12, f32[32,128]{1,0:T(8,128)S(1)} %copy-done.2, bf16[32,128,128]{2,1,0:T(8,128)(2,1)} %bitcast.61, pred[32,128]{1,0:T(8,128)(4,1)S(1)} %compare_and_fusion), kind=kLoop, calls=%fused_computation.15 | loop fusion | flops 3145728 | bytes 3166208 | tf_op jit(solution)/shard_map/convert_element_type | solution.py:19
  50.3 6.5 %while.10 = (s32[]{:T(128)}, f32[2,32,4096]{2,1,0:T(8,128)}, bf16[2,4096,128]{2,1,0:T(8,128)(2,1)S(1)}, bf16[1024,128]{1,0:T(8,128)(2,1)S(1)}, s32[]{:T(128)}) while((s32[]{:T(128)}, f32[2,32,4096]{2,1,0:T(8,128)}, bf16[2,4096,128]{2,1,0:T(8,128)(2,1)S(1)}, bf16[1024,128]{1,0:T(8,128)(2,1)S(1)}, s32[]{:T(128)}) %tuple.30), condition=%wide.region_7.8_spmd, body=%wide.region_5.7_spmd.sunk | while | flops 1077805056 | bytes 2884161 | solution.py:54
  50.3 2.4 %bitcast_reduce_fusion.2 = f32[32,4096]{1,0:T(8,128)S(1)} fusion(bf16[1024,128]{1,0:T(8,128)(2,1)S(1)} %get-tuple-element.79, bf16[2,4096,128]{2,1,0:T(8,128)(2,1)S(1)} %get-tuple-element.78, s32[]{:T(128)} %get-tuple-element.71), kind=kOutput, calls=%fused_computation.2.clone.1 | convolution fusion | flops 1077805056 | bytes 1835012 | tf_op jit(solution)/shard_map/while/body/eval_jaxpr/dot_general | solution.py:49
  52.7 0.9 bitcast_dynamic-update-slice_fusion.2
  53.6 2.4 %bitcast_reduce_fusion.2 = f32[32,4096]{1,0:T(8,128)S(1)} fusion(bf16[1024,128]{1,0:T(8,128)(2,1)S(1)} %get-tuple-element.79, bf16[2,4096,128]{2,1,0:T(8,128)(2,1)S(1)} %get-tuple-element.78, s32[]{:T(128)} %get-tuple-element.71), kind=kOutput, calls=%fused_computation.2.clone.1 | convolution fusion | flops 1077805056 | bytes 1835012 | tf_op jit(solution)/shard_map/while/body/eval_jaxpr/dot_general | solution.py:49
  55.9 0.9 bitcast_dynamic-update-slice_fusion.2
  57.3 0.7 reduce.6
  58.1 4.9 %fusion.8 = bf16[64,8,128,128]{3,1,2,0:T(8,128)(2,1)S(1)} fusion(bf16[4,8,128,128]{3,2,1,0:T(8,128)(2,1)S(1)} %bitcast.60, s32[512]{0:T(512)S(1)} %eq.60), kind=kOutput, calls=%fused_computation.12 | convolution fusion | flops 545275904 | bytes 17827840 | tf_op jit(solution)/shard_map/dot_general | solution.py:25
  63.1 8.4 %copy.33 = bf16[64,8,128,128]{3,2,1,0:T(8,128)(2,1)} copy(bf16[64,8,128,128]{3,1,2,0:T(8,128)(2,1)S(1)} %fusion.8) | data formatting | bytes 33554432
  71.8 55.6 %all-to-all-done.1 = bf16[32,16,32,128]{3,2,1,0:T(8,128)(2,1)} async-done(((bf16[32,16,32,128]{3,2,1,0:T(8,128)(2,1)}), bf16[32,16,32,128]{3,2,1,0:T(8,128)(2,1)}, u32[]{:S(2)}, u32[]{:S(2)}) %all-to-all-start.1) | async-done | bytes 4194336 | tf_op jit(solution)/shard_map/all_to_all | solution.py:89
  127.3 13.1 %select_reduce_fusion = f32[32,16,32]{2,1,0:T(8,128)S(1)} fusion(pred[32,16,128]{2,1,0:T(8,128)(4,1)S(1)} %iota_compare_fusion.4, bf16[32,16,32,128]{3,2,1,0:T(8,128)(2,1)} %all-to-all-done.1, bf16[32,16,128,128]{3,2,1,0:T(8,128)(2,1)} %bitcast.57), kind=kOutput, calls=%fused_computation.11 | convolution fusion | flops 541048832 | bytes 21102592 | tf_op jit(solution)/shard_map/sctd,scpd->sctp/dot_general | solution.py:93
  141.2 2.6 %all-to-all-start.2 = ((f32[32,1,16]{2,1,0:T(1,128)}), f32[32,1,16]{2,1,0:T(1,128)S(1)}, u32[]{:S(2)}, u32[]{:S(2)}) async-start(f32[32,1,16]{2,1,0:T(1,128)} %bitcast.9), calls=%async_computation.2 | async-start | bytes 32768 | tf_op jit(solution)/shard_map/all_to_all | solution.py:94
  143.8 2.3 %copy.29 = f32[2,4,8,4096]{3,2,0,1:T(8,128)} copy(f32[2,4,8,4096]{3,2,1,0:T(8,128)} %bitcast.17) | data formatting | bytes 2097152 | tf_op jit(solution)/shard_map/reshape | solution.py:54
  146.1 4.9 %all-to-all-done.2 = f32[32,1,16]{2,1,0:T(1,128)S(1)} async-done(((f32[32,1,16]{2,1,0:T(1,128)}), f32[32,1,16]{2,1,0:T(1,128)S(1)}, u32[]{:S(2)}, u32[]{:S(2)}) %all-to-all-start.2) | async-done | bytes 2080 | tf_op jit(solution)/shard_map/all_to_all | solution.py:94
  152.2 1.9 %gather_fusion.1 = f32[256]{0:T(256)S(1)} fusion(f32[512]{0:T(512)S(1)} %reshape.163, s32[1024]{0:T(1024)S(1)} %pad_clamp_fusion), kind=kCustom, calls=%fused_computation.1 | custom fusion | bytes 3072 | tf_op jit(solution)/shard_map/gather | solution.py:101
  (38 shorter events, 4.5 us)
Async XLA Ops:
  3.4 22.5 %all-to-all-start = ((s32[32,1,16]{2,1,0:T(1,128)}), s32[32,1,16]{2,1,0:T(1,128)S(1)}, u32[]{:S(2)}, u32[]{:S(2)}) async-start(s32[32,1,16]{2,1,0:T(1,128)} %bitcast.4), calls=%async_computation | async-start | bytes 32768 | tf_op jit(solution)/shard_map/all_to_all | solution.py:88
  25.9 5.9 %copy-start.3 = (s32[1,32,8]{1,2,0:T(8,128)S(1)}, s32[1,32,8]{1,2,0:T(8,128)}, u32[]{:S(2)}) copy-start(s32[1,32,8]{1,2,0:T(8,128)} %param.16) | copy-start | bytes 3076
  25.9 6.1 %copy-start.1 = (s32[32,128]{1,0:T(8,128)S(1)}, s32[32,128]{1,0:T(8,128)}, u32[]{:S(2)}) copy-start(s32[32,128]{1,0:T(8,128)} %param.14) | copy-start | bytes 49156
  25.9 6.1 %copy-start = (bf16[8192,128]{1,0:T(8,128)(2,1)S(1)}, bf16[8192,128]{1,0:T(8,128)(2,1)}, u32[]{:S(2)}) copy-start(bf16[8192,128]{1,0:T(8,128)(2,1)} %param.11) | copy-start | bytes 6291460
  25.9 101.4 %all-to-all-start.1 = ((bf16[32,16,32,128]{3,2,1,0:T(8,128)(2,1)}), bf16[32,16,32,128]{3,2,1,0:T(8,128)(2,1)}, u32[]{:S(2)}, u32[]{:S(2)}) async-start(bf16[32,16,32,128]{3,2,1,0:T(8,128)(2,1)} %bitcast.59), calls=%async_computation.1 | async-start | bytes 8388608 | tf_op jit(solution)/shard_map/all_to_all | solution.py:89
  32.0 15.1 %copy-start.2 = (f32[32,128]{1,0:T(8,128)S(1)}, f32[32,128]{1,0:T(8,128)}, u32[]{:S(2)}) copy-start(f32[32,128]{1,0:T(8,128)} %param.13) | copy-start | bytes 49156
  63.1 8.4 %copy-start.4 = (s32[32]{0:T(128)S(1)}, s32[32]{0:T(128)}, u32[]{:S(2)}) copy-start(s32[32]{0:T(128)} %param.15) | copy-start | bytes 388
  141.2 9.7 %all-to-all-start.2 = ((f32[32,1,16]{2,1,0:T(1,128)}), f32[32,1,16]{2,1,0:T(1,128)S(1)}, u32[]{:S(2)}, u32[]{:S(2)}) async-start(f32[32,1,16]{2,1,0:T(1,128)} %bitcast.9), calls=%async_computation.2 | async-start | bytes 32768 | tf_op jit(solution)/shard_map/all_to_all | solution.py:94
where the time goes:
time: 155 us
  waiting for transfers between devices  60.4 us (39%)
  local copies, waits for them, and re-layouts  39.4 us (25%)
  matrix products  26.4 us (17%)
  starting transfers between devices  15.7 us (10%)
  blocking collectives  6.34 us (4%)
  other arithmetic  5.71 us (4%)
    all_to_all x1, waiting for transfers between devices, per_device(): lax.all_to_all(outgoing, ('lists', 'score'), split_axis=0, concat_axis=0,...  55.6 us
    unnamed x15, local copies, waits for them, and re-layouts  16 us
    gather x1, local copies, waits for them, and re-layouts, rebuild_held(): jnp.take(centroids, centroid_ids.reshape(-1), axis=0).astype(jnp.float32)  15 us
    dot_general x1, matrix products, per_device(): jnp.einsum('sctd,scpd->sctp', asked, vectors, preferred_element_type=jnp....  13.1 us
    all_to_all x1, starting transfers between devices, per_device(): lax.all_to_all(request, ('lists', 'score'), split_axis=0, concat_axis=0,...  7.33 us
    all_gather x1, blocking collectives, per_device(): gathered = lax.all_gather(queries, 'lists', axis=1, tiled=True)  6.34 us
    all_to_all x1, starting transfers between devices, per_device(): lax.all_to_all(outgoing, ('lists', 'score'), split_axis=0, concat_axis=0,...  5.83 us
    dot_general x1, matrix products, pick_blocks(): jnp.dot(picker.astype(jnp.bfloat16), held_vectors, preferred_element_type...  4.94 us
  transfers between devices with their start and end apart: 3, of which 2 were waited for; matrix products, arithmetic and copies ran while one was open for 33% of the time, Pallas kernels for 0%

commit v1 on v0

v1 whole, which is shorter than its diff:
```python
import functools

import jax
import jax.numpy as jnp
from jax import lax
from jax.experimental import pallas as pl
from jax.experimental.pallas import tpu as pltpu
from jax.sharding import PartitionSpec as P

PAIRS = 16
ROWS = 16
AXES = ("lists", "score")


def score_kernel(
    ids_ref, lens_ref, pickq_ref, picks_ref, cent_ref, codes_ref, scales_ref, q_ref, out_ref, wide, base, vecs
):
    held, slot_len, width = codes_ref.shape
    cent_rows = cent_ref.shape[0]
    step = 512

    @pl.loop(0, cent_rows // step)
    def _(i):
        rows = pl.ds(pl.multiple_of(i * step, step), step)
        wide[rows, :] = cent_ref[rows, :].astype(jnp.float32)

    @pl.loop(0, held)
    def _(b):
        @pl.loop(0, (lens_ref[b] + ROWS - 1) // ROWS)
        def _(r):
            first = pl.multiple_of(r * ROWS, ROWS)
            for j in range(ROWS):
                base[pl.ds(first + j, 1), :] = wide[pl.ds(ids_ref[b, first + j], 1), :]

        row = scales_ref[pl.ds(b, 1), :]
        spread = jnp.transpose(jnp.broadcast_to(row, (slot_len, slot_len)))
        if width != slot_len:
            spread = jnp.broadcast_to(spread[:, :1], (slot_len, width))
        vecs[b] = (base[...] + spread * codes_ref[b].astype(jnp.float32)).astype(jnp.bfloat16)

    lanes = lax.broadcasted_iota(jnp.int32, (1, slot_len), 1)

    @pl.loop(0, out_ref.shape[0])
    def _(i):
        acc = jnp.zeros((1, 128), jnp.float32)
        spots = lax.broadcasted_iota(jnp.int32, (1, 128), 1)
        for j in range(PAIRS):
            slot = picks_ref[i * PAIRS + j]
            inner = lax.dot_general(
                q_ref[pickq_ref[i * PAIRS + j]],
                vecs[slot],
                (((1,), (1,)), ((), ())),
                preferred_element_type=jnp.float32,
            )
            inner = jnp.where(lanes < lens_ref[slot], inner, -1e30)
            best = jnp.max(inner, axis=1, keepdims=True)
            total = jnp.sum(best, axis=0, keepdims=True)
            acc = jnp.where(spots == j, total, acc)
        out_ref[pl.ds(i, 1), :] = acc * (1.0 / q_ref.shape[1])


def score_pairs(ids, lens, pickq, picks, centroids, codes, scales, allq):
    held, slot_len, width = codes.shape
    smem = pl.BlockSpec(memory_space=pltpu.SMEM)
    vmem = pl.BlockSpec(memory_space=pltpu.VMEM)
    return pl.pallas_call(
        score_kernel,
        out_shape=jax.ShapeDtypeStruct((pickq.shape[0] // PAIRS, 128), jnp.float32),
        in_specs=[smem] * 4 + [vmem] * 4,
        out_specs=vmem,
        scratch_shapes=[
            pltpu.VMEM(centroids.shape, jnp.float32),
            pltpu.VMEM((slot_len, width), jnp.float32),
            pltpu.VMEM(codes.shape, jnp.bfloat16),
        ],
        compiler_params=pltpu.CompilerParams(vmem_limit_bytes=40 * 1024 * 1024),
    )(ids, lens, pickq, picks, centroids, codes, scales, allq)


def before(count):
    spots = jnp.arange(count, dtype=jnp.int32)
    return (spots[:, None] < spots[None, :]).astype(jnp.bfloat16)


def per_device(queries, centroids, codes, scales, centroid_ids, lengths, owners, slots):
    lists, score = lax.axis_size("lists"), lax.axis_size("score")
    devices = lists * score
    me = lax.axis_index("lists") * score + lax.axis_index("score")
    query_rows, per_query = owners.shape[1:]
    capacity = max(4, 2 * -(-query_rows * per_query // devices))
    held = codes.shape[0]

    mine = lax.all_gather(queries, "lists", axis=1, tiled=True)
    allq = lax.all_gather(mine, "score", axis=0, tiled=True)
    token_count, width = mine.shape[1:]
    asked = lax.all_gather(owners[0] * held + slots[0], AXES, axis=0)

    inner = lax.dot_general(
        mine.reshape(-1, width), centroids, (((1,), (1,)), ((), ())), preferred_element_type=jnp.float32
    )
    relevance = jnp.max(inner.reshape(query_rows, token_count, -1), axis=1)

    hit = asked // held == me
    named = jnp.any(hit, axis=2)
    slot = jnp.sum(jnp.where(hit, asked % held, 0), axis=2)
    place = jnp.dot(named.astype(jnp.bfloat16), before(query_rows), preferred_element_type=jnp.float32).astype(jnp.int32)
    take = named[:, None, :] & (place[:, None, :] == jnp.arange(capacity, dtype=jnp.int32)[None, :, None])
    group = jnp.arange(devices, dtype=jnp.int32) % score
    query = group[:, None] * query_rows + jnp.arange(query_rows, dtype=jnp.int32)[None, :]
    pickq = jnp.sum(jnp.where(take, query[:, None, :], 0), axis=2).reshape(-1)
    picks = jnp.sum(jnp.where(take, slot[:, None, :], 0), axis=2).reshape(-1)

    done = score_pairs(centroid_ids, lengths, pickq, picks, centroids, codes, scales, allq)
    done = done[:, :PAIRS].reshape(devices, capacity)
    full = jnp.sum(jnp.where(take, done[:, :, None], 0.0), axis=1)
    back = lax.all_to_all(full, AXES, split_axis=0, concat_axis=0, tiled=True)
    which = owners[0][:, :, None] == jnp.arange(devices, dtype=jnp.int32)
    scores = jnp.sum(jnp.where(which, jnp.transpose(back)[:, None, :], 0.0), axis=2)
    return (scores[None], relevance)


def solution(mesh):
    placed = (
        P("score", "lists", None),
        P("lists", None),
        P(("lists", "score"), None, None),
        P(("lists", "score"), None),
        P(("lists", "score"), None),
        P(("lists", "score")),
        P("lists", "score", None),
        P("lists", "score", None),
    )
    return jax.shard_map(
        per_device,
        mesh=mesh,
        in_specs=placed,
        out_specs=(P("lists", "score", None), P("score", "lists")),
        check_vma=False,
    )
```

time: 155 us -> 139 us (0.90)
  blocking collectives: 6.34 us -> 78.1 us
  waiting for transfers between devices: 60.4 us -> 1.27 us
  local copies, waits for them, and re-layouts: 39.4 us -> 7.48 us
  Pallas kernels: 0 us -> 26.6 us
  matrix products: 26.4 us -> 5.9 us
  between operations: 0.84 us -> 14.1 us
  starting transfers between devices: 15.7 us -> 2.6 us
  other arithmetic: 5.71 us -> 3.12 us
    all_gather x1 -> x2, blocking collectives: 6.34 us -> 78.1 us  [the longest x1 69.2 us: per_device(): asked = lax.all_gather(owners[0] * held + slots[0], AXES, axis=0)]
    all_to_all x3 -> x1, waiting for transfers between devices: 60.4 us -> 1.25 us  [per_device(): back = lax.all_to_all(full, AXES, split_axis=0, concat_axis=0, tiled=True)]
    pallas_call x0 -> x1, Pallas kernels: none -> 26.6 us  [score_pairs(): pl.pallas_call(score_kernel, out_shape=jax.ShapeDtypeStruct((pickq.shape[...]
    dot_general x6 -> x2, matrix products: 26.4 us -> 5.9 us  [the longest x1 5.78 us: per_device(): lax.dot_general(mine.reshape(-1, width), centroids, (((1,), (1,)), ((), (...]
    gather x2 -> x0, local copies, waits for them, and re-layouts: 17 us -> none  [the longest x1 15 us: rebuild_held(): jnp.take(centroids, centroid_ids.reshape(-1), axis=0).astype(jnp.float32)]
    all_to_all x3 -> x1, starting transfers between devices: 15.7 us -> 2.57 us  [per_device(): back = lax.all_to_all(full, AXES, split_axis=0, concat_axis=0, tiled=True)]
    unnamed x15 -> x19, local copies, waits for them, and re-layouts: 16 us -> 7.18 us
    convert_element_type x2 -> x0, other arithmetic: 3.16 us -> none  [the longest x1 3.16 us: rebuild_held(): return vectors.astype(jnp.bfloat16).reshape(held, slot_len * width)]
  transfers between devices with their start and end apart: 3 -> 2, of which waited for: 2 -> 1; matrix products, arithmetic and copies ran while one was open for 33% -> 6% of each run, Pallas kernels for 0% -> 0%
where the time goes in v1:
time: 139 us
  blocking collectives  78.1 us (56%)
  Pallas kernels  26.6 us (19%)
  between operations  14.1 us (10%)
  local copies, waits for them, and re-layouts  7.48 us (5%)
  matrix products  5.9 us (4%)
  other arithmetic  3.12 us (2%)
  starting transfers between devices  2.6 us (2%)
    all_gather x1, blocking collectives, per_device(): asked = lax.all_gather(owners[0] * held + slots[0], AXES, axis=0)  69.2 us
    pallas_call x1, Pallas kernels, score_pairs(): pl.pallas_call(score_kernel, out_shape=jax.ShapeDtypeStruct((pickq.shape[...  26.6 us
    all_gather x1, blocking collectives, per_device(): mine = lax.all_gather(queries, 'lists', axis=1, tiled=True)  8.88 us
    unnamed x19, local copies, waits for them, and re-layouts  7.18 us
    dot_general x1, matrix products, per_device(): lax.dot_general(mine.reshape(-1, width), centroids, (((1,), (1,)), ((), (...  5.78 us
  transfers between devices with their start and end apart: 2, of which 1 were waited for; matrix products, arithmetic and copies ran while one was open for 6% of the time, Pallas kernels for 0%

profile of v1, /device:TPU:0, one launch (start us, length us, event | category | flops | bytes accessed | tf_op | source)
XLA Modules:
  0.0 139.2 jit_solution(2139647158384601515)
XLA Ops:
  7.2 8.9 %all_gather.11 = bf16[32,32,128]{2,1,0:T(8,128)(2,1)} all-gather(bf16[32,8,128]{2,1,0:T(8,128)(2,1)} %param.8), channel_id=1, replica_groups=mesh['lists'=4,'score'=8] {'lists'}, dimensions={1}, use_global_device_ids=true | all-gather | bytes 327680 | tf_op jit(solution)/shard_map/all_gather | solution.py:93
  16.1 0.7 multiply_add_fusion
  16.8 69.2 %all_gather.10 = s32[32,32,8]{1,2,0:T(8,128)S(1)} all-gather(s32[1,32,8]{1,2,0:T(8,128)S(1)} %multiply_add_fusion), channel_id=1, replica_groups=mesh['lists'=4,'score'=8] {'lists','score'}, dimensions={0}, use_global_device_ids=true | all-gather | bytes 33792 | tf_op jit(solution)/shard_map/all_gather | solution.py:96
  86.1 0.1 fusion.8
  86.2 0.1 fusion.4
  86.3 0.1 iota_add_fusion
  86.4 0.1 convolution_convert_fusion
  86.5 1.2 select_reduce_fusion.1
  87.7 0.1 reshape.50.pickq_ref
  87.8 0.1 reshape.51.picks_ref
  87.9 1.6 %copy-done = bf16[8192,128]{1,0:T(8,128)(2,1)S(1)} copy-done((bf16[8192,128]{1,0:T(8,128)(2,1)S(1)}, bf16[8192,128]{1,0:T(8,128)(2,1)}, u32[]{:S(2)}) %copy-start) | copy-done | bytes 2097176
  89.5 1.6 %copy-done.2 = bf16[256,32,128]{2,1,0:T(8,128)(2,1)S(1)} copy-done((bf16[256,32,128]{2,1,0:T(8,128)(2,1)S(1)}, bf16[256,32,128]{2,1,0:T(8,128)(2,1)}, u32[]{:S(2)}) %copy-start.2) | copy-done | bytes 2097176
  91.1 1.2 copy-done.3
  92.3 0.7 copy-done.4
  93.0 0.7 copy-done.5
  93.7 0.7 copy-done.6
  94.4 26.6 %shard_map.95 = f32[32,128]{1,0:T(8,128)S(1)} custom-call(s32[32,128]{1,0:T(8,128)S(1)} %copy-done.4, s32[32]{0:T(128)S(1)} %copy-done.6, s32[512]{0:T(512)S(1)} %reshape.50.pickq_ref, s32[512]{0:T(512)S(1)} %reshape.51.picks_ref, bf16[8192,128]{1,0:T(8,128)(2,1)S(1)} %copy-done, bf16[32,128,128]{2,1,0:T(8,128)(2,1)S(1)} %copy-done.3, ...), custom_call_target="tpu_custom_call" | custom-call | tf_op jit(solution)/shard_map/pallas_call | solution.py:66
  121.0 0.8 select_reduce_fusion
  121.8 2.6 %all-to-all-start = ((f32[32,1,32]{2,1,0:T(1,128)}), f32[32,1,32]{2,1,0:T(1,128)S(1)}, u32[]{:S(2)}, u32[]{:S(2)}) async-start(f32[32,1,32]{2,1,0:T(1,128)} %bitcast.2), calls=%async_computation | async-start | bytes 32768 | tf_op jit(solution)/shard_map/all_to_all | solution.py:116
  124.4 5.8 %convolution_reduce_fusion = f32[32,8192]{1,0:T(8,128)} fusion(bf16[32,32,128]{2,1,0:T(8,128)(2,1)S(1)} %copy-done.7, bf16[8192,128]{1,0:T(8,128)(2,1)S(1)} %copy-done.1), kind=kOutput, calls=%fused_computation | convolution fusion | flops 2155610112 | bytes 3407872 | tf_op jit(solution)/shard_map/dot_general | solution.py:98
  130.1 0.1 copy.14
  130.2 1.3 all-to-all-done
  131.5 0.2 select_reduce_fusion.3
  131.7 0.7 copy.17
  (17 shorter events, 0.2 us)
Async XLA Ops:
  7.2 80.7 %all-gather.2.cloned.1.call-start = ((), (), s32[]{:S(2)}) async-start(), calls=%async_computation.1 | async-start | bytes 2359296 | tf_op jit(solution)/shard_map/all_gather | solution.py:94
  87.9 1.6 %copy-start = (bf16[8192,128]{1,0:T(8,128)(2,1)S(1)}, bf16[8192,128]{1,0:T(8,128)(2,1)}, u32[]{:S(2)}) copy-start(bf16[8192,128]{1,0:T(8,128)(2,1)} %cent_ref.1) | copy-start | bytes 6291460
  89.5 1.6 %copy-start.2 = (bf16[256,32,128]{2,1,0:T(8,128)(2,1)S(1)}, bf16[256,32,128]{2,1,0:T(8,128)(2,1)}, u32[]{:S(2)}) copy-start(bf16[256,32,128]{2,1,0:T(8,128)(2,1)} %all-gather.2.cloned.1.call-done.q_ref) | copy-start | bytes 6291460
  91.1 1.2 copy-start.3
  92.3 0.7 copy-start.4
  93.0 0.7 copy-start.5
  93.7 0.7 copy-start.6
  94.4 30.0 %copy-start.1 = (bf16[8192,128]{1,0:T(8,128)(2,1)S(1)}, bf16[8192,128]{1,0:T(8,128)(2,1)}, u32[]{:S(2)}) copy-start(bf16[8192,128]{1,0:T(8,128)(2,1)} %cent_ref.1) | copy-start | bytes 6291460
  94.4 30.0 %copy-start.7 = (bf16[32,32,128]{2,1,0:T(8,128)(2,1)S(1)}, bf16[32,32,128]{2,1,0:T(8,128)(2,1)}, u32[]{:S(2)}) copy-start(bf16[32,32,128]{2,1,0:T(8,128)(2,1)} %all_gather.11) | copy-start | bytes 786436
  121.8 9.7 %all-to-all-start = ((f32[32,1,32]{2,1,0:T(1,128)}), f32[32,1,32]{2,1,0:T(1,128)S(1)}, u32[]{:S(2)}, u32[]{:S(2)}) async-start(f32[32,1,32]{2,1,0:T(1,128)} %bitcast.2), calls=%async_computation | async-start | bytes 32768 | tf_op jit(solution)/shard_map/all_to_all | solution.py:116
  124.4 5.8 %copy-start.8 = (s32[1,32,8]{1,2,0:T(8,128)S(1)}, s32[1,32,8]{1,2,0:T(8,128)}, u32[]{:S(2)}) copy-start(s32[1,32,8]{1,2,0:T(8,128)} %param.14) | copy-start | bytes 3076
Sparse Core Ops, SparseCore 0:
  16.2 50.0 all-gather.1

commit v2 on v1

--- a/solution.py
+++ b/solution.py
@@ -1,4 +1,6 @@
 import functools
+import itertools
+import math
 
 import jax
 import jax.numpy as jnp
@@ -77,6 +79,111 @@
     )(ids, lens, pickq, picks, centroids, codes, scales, allq)
 
 
+MESH = pl.DeviceIdType.MESH
+
+
+def split_sizes(lists, score):
+    core = 2 if lists % 2 == 0 else 1
+    inner = 2 if score <= 8 and score % 2 == 0 else math.gcd(score, 4)
+    return (score // inner, inner, lists // core, core)
+
+
+def spread_kernel(sizes, q_ref, asked_ref, allq_ref, all_asked_ref, send_sem, recv_sem, own_sem):
+    li, sc = lax.axis_index("lists"), lax.axis_index("score")
+    mine = (sc // sizes[1], sc % sizes[1], li // sizes[3], li % sizes[3])
+    rows = q_ref.shape[0]
+    half = rows // 2
+    score = sizes[0] * sizes[1]
+
+    def device(at):
+        return (at[2] * sizes[3] + at[3], at[0] * sizes[1] + at[1])
+
+    def moved(dim, by):
+        return tuple(lax.rem(c + by + n, n) if d == dim else c for d, (c, n) in enumerate(zip(mine, sizes)))
+
+    def block(part, back):
+        at = device([lax.rem(c - b + n, n) if b else c for c, b, n in zip(mine, back, sizes)])
+        if part == 2:
+            return all_asked_ref.at[at[0] * score + at[1]]
+        return allq_ref.at[pl.ds(at[1] * rows + part * half, half), at[0]]
+
+    def own(part):
+        return asked_ref if part == 2 else q_ref.at[pl.ds(part * half, half)]
+
+    barrier = pltpu.get_barrier_semaphore()
+    peers = [(d, by) for d in range(4) for by in range(1, sizes[d])]
+    for d, by in peers:
+        pl.semaphore_signal(barrier, inc=1, device_id=device(moved(d, by)), device_id_type=MESH)
+    pl.semaphore_wait(barrier, len(peers))
+
+    orders = ((0, 1, 2, 3), (0, 2, 1, 3), (0, 1, 2, 3))
+    places = list(itertools.product(*(range(n) for n in sizes)))
+    number = {back: i for i, back in enumerate(places)}
+
+    def cost(item):
+        part, back = item
+        return (sum((1 if d == 3 else 3 + b) for d, b in enumerate(back) if b), -part)
+
+    zero = (0, 0, 0, 0)
+    sent = []
+    own_copies = [pltpu.make_async_copy(own(p), block(p, zero), own_sem.at[p]) for p in range(3)]
+    for copy in own_copies:
+        copy.start()
+    for part, back in sorted(itertools.product(range(3), places), key=cost):
+        order = orders[part]
+        here = block(part, back)
+        last = max([order.index(d) for d in range(4) if back[d]], default=-1)
+        if back != zero:
+            pltpu.make_async_remote_copy(
+                src_ref=here,
+                dst_ref=here,
+                send_sem=send_sem.at[part, number[back]],
+                recv_sem=recv_sem.at[part, number[back]],
+                device_id=device(moved(order[last], 1)),
+                device_id_type=MESH,
+            ).wait_recv()
+        for d in order[last + 1 :]:
+            for by in range(1, sizes[d]):
+                there = number[tuple(by if e == d else b for e, b in enumerate(back))]
+                copy = pltpu.make_async_remote_copy(
+                    src_ref=own(part) if back == zero else here,
+                    dst_ref=here,
+                    send_sem=send_sem.at[part, there],
+                    recv_sem=recv_sem.at[part, there],
+                    device_id=device(moved(d, by)),
+                    device_id_type=MESH,
+                )
+                copy.start()
+                sent.append(copy)
+    for copy in sent:
+        copy.wait_send()
+    for copy in own_copies:
+        copy.wait()
+
+
+def spread(queries, asked, lists, score):
+    rows, tokens, width = queries.shape
+    vmem = pl.BlockSpec(memory_space=pltpu.VMEM)
+    devices = lists * score
+    return pl.pallas_call(
+        functools.partial(spread_kernel, split_sizes(lists, score)),
+        out_shape=[
+            jax.ShapeDtypeStruct((score * rows, lists, tokens, width), queries.dtype),
+            jax.ShapeDtypeStruct((devices,) + asked.shape, asked.dtype),
+        ],
+        in_specs=[vmem] * 2,
+        out_specs=[vmem] * 2,
+        scratch_shapes=[
+            pltpu.SemaphoreType.DMA((3, devices)),
+            pltpu.SemaphoreType.DMA((3, devices)),
+            pltpu.SemaphoreType.DMA((3,)),
+        ],
+        compiler_params=pltpu.CompilerParams(
+            collective_id=0, has_side_effects=True, vmem_limit_bytes=16 * 1024 * 1024
+        ),
+    )(queries, asked)
+
+
 def before(count):
     spots = jnp.arange(count, dtype=jnp.int32)
     return (spots[:, None] < spots[None, :]).astype(jnp.bfloat16)
@@ -90,10 +197,12 @@
     capacity = max(4, 2 * -(-query_rows * per_query // devices))
     held = codes.shape[0]
 
-    mine = lax.all_gather(queries, "lists", axis=1, tiled=True)
-    allq = lax.all_gather(mine, "score", axis=0, tiled=True)
-    token_count, width = mine.shape[1:]
-    asked = lax.all_gather(owners[0] * held + slots[0], AXES, axis=0)
+    named_here = (owners[0] * held + slots[0]).reshape(-1, 128)
+    allq, asked = spread(queries, named_here, lists, score)
+    token_count, width = lists * queries.shape[1], queries.shape[2]
+    allq = allq.reshape(score * query_rows, token_count, width)
+    asked = asked.reshape(devices, query_rows, per_query)
+    mine = lax.dynamic_slice_in_dim(allq, lax.axis_index("score") * query_rows, query_rows, 0)
 
     inner = lax.dot_general(
         mine.reshape(-1, width), centroids, (((1,), (1,)), ((), ())), preferred_element_type=jnp.float32

time: 139 us -> 74.1 us (0.53)
  blocking collectives: 78.1 us -> 0 us
  Pallas kernels: 26.6 us -> 48 us
  between operations: 14.1 us -> 0.73 us
  local copies, waits for them, and re-layouts: 7.48 us -> 10.1 us
  starting transfers between devices: 2.6 us -> 4.47 us
    all_gather x2 -> x0, blocking collectives: 78.1 us -> none  [the longest x1 69.2 us: per_device(): asked = lax.all_gather(owners[0] * held + slots[0], AXES, axis=0)]
    pallas_call x0 -> x1, Pallas kernels: none -> 22.6 us  [spread(): pl.pallas_call(functools.partial(spread_kernel, split_sizes(lists, score)...]
    unnamed x19 -> x21, local copies, waits for them, and re-layouts: 7.18 us -> 9.36 us
    all_to_all x1, starting transfers between devices: 2.57 us -> 4.47 us  [per_device(): back = lax.all_to_all(full, AXES, split_axis=0, concat_axis=0, tiled=True)]
  transfers between devices with their start and end apart: 2 -> 1, of which waited for: 1 -> 1; matrix products, arithmetic and copies ran while one was open for 6% -> 9% of each run, Pallas kernels for 0% -> 0%
where the time goes in v2:
time: 74.1 us; the launch traced here: 73.6 us
  Pallas kernels  48 us (65%)
  local copies, waits for them, and re-layouts  10.1 us (14%)
  matrix products  6.93 us (9%)
  starting transfers between devices  4.47 us (6%)
  other arithmetic  3.12 us (4%)
    pallas_call x1, Pallas kernels, score_pairs(): pl.pallas_call(score_kernel, out_shape=jax.ShapeDtypeStruct((pickq.shape[...  25.4 us
    pallas_call x1, Pallas kernels, spread(): pl.pallas_call(functools.partial(spread_kernel, split_sizes(lists, score)...  22.6 us
    unnamed x21, local copies, waits for them, and re-layouts  9.36 us
    dot_general x1, matrix products, per_device(): lax.dot_general(mine.reshape(-1, width), centroids, (((1,), (1,)), ((), (...  6.73 us
    all_to_all x1, starting transfers between devices, per_device(): back = lax.all_to_all(full, AXES, split_axis=0, concat_axis=0, tiled=True)  4.47 us
  transfers between devices with their start and end apart: 1, of which 1 were waited for; matrix products, arithmetic and copies ran while one was open for 9% of the time, Pallas kernels for 0%

profile of v2, /device:TPU:0, one launch (start us, length us, event | category | flops | bytes accessed | tf_op | source)
XLA Modules:
  0.0 73.6 jit_solution(15219547116520524742)
XLA Ops:
  0.6 0.7 multiply_add_fusion
  1.4 0.1 add.46.asked_ref
  1.5 0.8 %copy-done.5 = bf16[32,8,128]{2,1,0:T(8,128)(2,1)S(1)} copy-done((bf16[32,8,128]{2,1,0:T(8,128)(2,1)S(1)}, bf16[32,8,128]{2,1,0:T(8,128)(2,1)}, u32[]{:S(2)}) %copy-start.5) | copy-done | bytes 65560
  2.4 22.6 %shard_map.95 = (bf16[256,4,8,128]{3,2,1,0:T(8,128)(2,1)S(1)}, s32[32,2,128]{2,1,0:T(2,128)S(1)}) custom-call(bf16[32,8,128]{2,1,0:T(8,128)(2,1)S(1)} %copy-done.5, s32[2,128]{1,0:T(2,128)S(1)} %add.46.asked_ref), custom_call_target="tpu_custom_call" | custom-call | tf_op jit(solution)/shard_map/pallas_call | solution.py:168
  24.9 1.3 %copy-done.2 = bf16[256,4,8,128]{3,2,1,0:T(8,128)(2,1)} copy-done((bf16[256,4,8,128]{3,2,1,0:T(8,128)(2,1)}, bf16[256,4,8,128]{3,2,1,0:T(8,128)(2,1)S(1)}, u32[]{:S(2)}) %copy-start.2) | copy-done | bytes 2097176
  26.3 0.1 copy.23
  26.4 0.1 fusion.10
  26.5 0.2 convolution_convert_fusion
  26.7 0.1 copy.24
  26.8 0.1 fusion.5
  27.1 1.2 %select_reduce_fusion.1 = (s32[32,16]{1,0:T(8,128)S(1)}, s32[32,16]{1,0:T(8,128)S(1)}) fusion(s32[32,32]{1,0:T(8,128)S(1)} %copy.25, s32[32,32]{1,0:T(8,128)S(1)} %convolution_convert_fusion, pred[32,32]{1,0:T(8,128)(4,1)S(1)} %copy.24, s32[32,32]{1,0:T(8,128)S(1)} %iota_add_fusion), kind=kLoop, calls=%fused_computation.5 | loop fusion | flops 97280 | bytes 17408 | tf_op jit(solution)/shard_map/reduce_sum | solution.py:220
  28.4 1.6 %copy-done = bf16[8192,128]{1,0:T(8,128)(2,1)S(1)} copy-done((bf16[8192,128]{1,0:T(8,128)(2,1)S(1)}, bf16[8192,128]{1,0:T(8,128)(2,1)}, u32[]{:S(2)}) %copy-start) | copy-done | bytes 2097176
  30.0 1.6 %copy-done.3 = bf16[256,4,8,128]{3,2,1,0:T(8,128)(2,1)S(1)} copy-done((bf16[256,4,8,128]{3,2,1,0:T(8,128)(2,1)S(1)}, bf16[256,4,8,128]{3,2,1,0:T(8,128)(2,1)}, u32[]{:S(2)}) %copy-start.3) | copy-done | bytes 2097176
  31.6 1.2 %copy-done.4 = bf16[32,128,128]{2,1,0:T(8,128)(2,1)S(1)} copy-done((bf16[32,128,128]{2,1,0:T(8,128)(2,1)S(1)}, bf16[32,128,128]{2,1,0:T(8,128)(2,1)}, u32[]{:S(2)}) %copy-start.4) | copy-done | bytes 1048600
  32.8 0.7 copy-done.6
  33.5 0.7 copy-done.7
  34.3 0.7 copy-done.8
  34.9 25.4 %shard_map.96 = f32[32,128]{1,0:T(8,128)S(1)} custom-call(s32[32,128]{1,0:T(8,128)S(1)} %copy-done.6, s32[32]{0:T(128)S(1)} %copy-done.8, s32[512]{0:T(512)S(1)} %reshape.63.pickq_ref, s32[512]{0:T(512)S(1)} %reshape.64.picks_ref, bf16[8192,128]{1,0:T(8,128)(2,1)S(1)} %copy-done, bf16[32,128,128]{2,1,0:T(8,128)(2,1)S(1)} %copy-done.4, ...), custom_call_target="tpu_custom_call" | custom-call | tf_op jit(solution)/shard_map/pallas_call | solution.py:68
  60.3 0.8 %select_reduce_fusion = f32[32,32]{1,0:T(8,128)} fusion(f32[32,16]{1,0:T(8,128)S(1)} %bitcast.17, s32[32,32]{1,0:T(8,128)S(1)} %convolution_convert_fusion, pred[32,32]{1,0:T(8,128)(4,1)S(1)} %copy.24), kind=kLoop, calls=%fused_computation.4 | loop fusion | flops 64512 | bytes 11264 | tf_op jit(solution)/shard_map/reduce_sum | solution.py:224
  61.1 4.5 %all-to-all-start = ((f32[32,1,32]{2,1,0:T(1,128)}), f32[32,1,32]{2,1,0:T(1,128)S(1)}, u32[]{:S(2)}, u32[]{:S(2)}) async-start(f32[32,1,32]{2,1,0:T(1,128)} %bitcast.4), calls=%async_computation | async-start | bytes 32768 | tf_op jit(solution)/shard_map/all_to_all | solution.py:225
  65.6 6.7 %convolution_reduce_fusion = f32[32,8192]{1,0:T(8,128)} fusion(bf16[8192,128]{1,0:T(8,128)(2,1)S(1)} %copy-done.1, bf16[256,32,128]{2,1,0:T(8,128)(2,1)} %bitcast.15, s32[]{:T(128)S(6)} %select_n.52), kind=kOutput, calls=%fused_computation | convolution fusion | flops 2155610112 | bytes 3407876 | tf_op jit(solution)/shard_map/dot_general | solution.py:207
  72.4 0.3 all-to-all-done
  72.8 0.2 select_reduce_fusion.3
  73.0 0.7 copy.28
  (20 shorter events, 0.6 us)
Async XLA Ops:
  1.5 0.8 %copy-start.5 = (bf16[32,8,128]{2,1,0:T(8,128)(2,1)S(1)}, bf16[32,8,128]{2,1,0:T(8,128)(2,1)}, u32[]{:S(2)}) copy-start(bf16[32,8,128]{2,1,0:T(8,128)(2,1)} %q_ref.1) | copy-start | bytes 196612
  24.9 1.4 %copy-start.2 = (bf16[256,4,8,128]{3,2,1,0:T(8,128)(2,1)}, bf16[256,4,8,128]{3,2,1,0:T(8,128)(2,1)S(1)}, u32[]{:S(2)}) copy-start(bf16[256,4,8,128]{3,2,1,0:T(8,128)(2,1)S(1)} %get-tuple-element.5) | copy-start | bytes 6291460
  28.4 1.6 %copy-start = (bf16[8192,128]{1,0:T(8,128)(2,1)S(1)}, bf16[8192,128]{1,0:T(8,128)(2,1)}, u32[]{:S(2)}) copy-start(bf16[8192,128]{1,0:T(8,128)(2,1)} %cent_ref.1) | copy-start | bytes 6291460
  30.0 1.6 %copy-start.3 = (bf16[256,4,8,128]{3,2,1,0:T(8,128)(2,1)S(1)}, bf16[256,4,8,128]{3,2,1,0:T(8,128)(2,1)}, u32[]{:S(2)}) copy-start(bf16[256,4,8,128]{3,2,1,0:T(8,128)(2,1)} %copy-done.2) | copy-start | bytes 6291460
  31.6 1.2 %copy-start.4 = (bf16[32,128,128]{2,1,0:T(8,128)(2,1)S(1)}, bf16[32,128,128]{2,1,0:T(8,128)(2,1)}, u32[]{:S(2)}) copy-start(bf16[32,128,128]{2,1,0:T(8,128)(2,1)} %codes_ref.1) | copy-start | bytes 3145732
  32.8 0.7 copy-start.6
  33.5 0.7 copy-start.7
  34.3 0.7 copy-start.8
  34.9 30.7 %copy-start.1 = (bf16[8192,128]{1,0:T(8,128)(2,1)S(1)}, bf16[8192,128]{1,0:T(8,128)(2,1)}, u32[]{:S(2)}) copy-start(bf16[8192,128]{1,0:T(8,128)(2,1)} %cent_ref.1) | copy-start | bytes 6291460
  61.1 11.6 %all-to-all-start = ((f32[32,1,32]{2,1,0:T(1,128)}), f32[32,1,32]{2,1,0:T(1,128)S(1)}, u32[]{:S(2)}, u32[]{:S(2)}) async-start(f32[32,1,32]{2,1,0:T(1,128)} %bitcast.4), calls=%async_computation | async-start | bytes 32768 | tf_op jit(solution)/shard_map/all_to_all | solution.py:225
  65.6 6.7 %copy-start.9 = (s32[1,32,8]{1,2,0:T(8,128)S(1)}, s32[1,32,8]{1,2,0:T(8,128)}, u32[]{:S(2)}) copy-start(s32[1,32,8]{1,2,0:T(8,128)} %param.14) | copy-start | bytes 3076

commit v3 on v2

--- a/solution.py
+++ b/solution.py
@@ -14,21 +14,21 @@
 AXES = ("lists", "score")
 
 
-def score_kernel(
-    ids_ref, lens_ref, pickq_ref, picks_ref, cent_ref, codes_ref, scales_ref, q_ref, out_ref, wide, base, vecs
-):
-    held, slot_len, width = codes_ref.shape
-    cent_rows = cent_ref.shape[0]
+def widen(cent, wide):
     step = 512
 
-    @pl.loop(0, cent_rows // step)
+    @pl.loop(0, cent.shape[0] // step)
     def _(i):
         rows = pl.ds(pl.multiple_of(i * step, step), step)
-        wide[rows, :] = cent_ref[rows, :].astype(jnp.float32)
-
-    @pl.loop(0, held)
+        wide[rows, :] = cent[rows, :].astype(jnp.float32)
+
+
+def rebuild(first_block, blocks, ids_ref, scales_ref, codes, wide, base, vecs_ref):
+    held, slot_len, width = codes.shape
+
+    @pl.loop(first_block, first_block + blocks)
     def _(b):
-        @pl.loop(0, (lens_ref[b] + ROWS - 1) // ROWS)
+        @pl.loop(0, slot_len // ROWS)
         def _(r):
             first = pl.multiple_of(r * ROWS, ROWS)
             for j in range(ROWS):
@@ -38,8 +38,11 @@
         spread = jnp.transpose(jnp.broadcast_to(row, (slot_len, slot_len)))
         if width != slot_len:
             spread = jnp.broadcast_to(spread[:, :1], (slot_len, width))
-        vecs[b] = (base[...] + spread * codes_ref[b].astype(jnp.float32)).astype(jnp.bfloat16)
-
+        vecs_ref[b] = (base[...] + spread * codes[b].astype(jnp.float32)).astype(jnp.bfloat16)
+
+
+def score_kernel(lens_ref, picks_ref, vecs, q_ref, out_ref):
+    held, slot_len, width = vecs.shape
     lanes = lax.broadcasted_iota(jnp.int32, (1, slot_len), 1)
 
     @pl.loop(0, out_ref.shape[0])
@@ -47,9 +50,10 @@
         acc = jnp.zeros((1, 128), jnp.float32)
         spots = lax.broadcasted_iota(jnp.int32, (1, 128), 1)
         for j in range(PAIRS):
-            slot = picks_ref[i * PAIRS + j]
+            pick = picks_ref[i * PAIRS + j]
+            slot = lax.rem(pick, held)
             inner = lax.dot_general(
-                q_ref[pickq_ref[i * PAIRS + j]],
+                q_ref[lax.div(pick, held)],
                 vecs[slot],
                 (((1,), (1,)), ((), ())),
                 preferred_element_type=jnp.float32,
@@ -61,22 +65,16 @@
         out_ref[pl.ds(i, 1), :] = acc * (1.0 / q_ref.shape[1])
 
 
-def score_pairs(ids, lens, pickq, picks, centroids, codes, scales, allq):
-    held, slot_len, width = codes.shape
+def score_pairs(lens, picks, vecs, allq):
     smem = pl.BlockSpec(memory_space=pltpu.SMEM)
     vmem = pl.BlockSpec(memory_space=pltpu.VMEM)
     return pl.pallas_call(
         score_kernel,
-        out_shape=jax.ShapeDtypeStruct((pickq.shape[0] // PAIRS, 128), jnp.float32),
-        in_specs=[smem] * 4 + [vmem] * 4,
+        out_shape=jax.ShapeDtypeStruct((picks.shape[0] // PAIRS, 128), jnp.float32),
+        in_specs=[smem] * 2 + [vmem] * 2,
         out_specs=vmem,
-        scratch_shapes=[
-            pltpu.VMEM(centroids.shape, jnp.float32),
-            pltpu.VMEM((slot_len, width), jnp.float32),
-            pltpu.VMEM(codes.shape, jnp.bfloat16),
-        ],
-        compiler_params=pltpu.CompilerParams(vmem_limit_bytes=40 * 1024 * 1024),
-    )(ids, lens, pickq, picks, centroids, codes, scales, allq)
+        compiler_params=pltpu.CompilerParams(vmem_limit_bytes=24 * 1024 * 1024),
+    )(lens, picks, vecs, allq)
 
 
 MESH = pl.DeviceIdType.MESH
@@ -88,7 +86,13 @@
     return (score // inner, inner, lists // core, core)
 
 
-def spread_kernel(sizes, q_ref, asked_ref, allq_ref, all_asked_ref, send_sem, recv_sem, own_sem):
+def spread_kernel(
+    sizes, q_ref, asked_ref, ids_ref, scales_ref, cent_hbm, codes_hbm, allq_ref, all_asked_ref, vecs_ref,
+    cent, codes, wide, base, send_sem, recv_sem, own_sem, load_sem,
+):
+    loads = [pltpu.make_async_copy(cent_hbm, cent, load_sem.at[0]), pltpu.make_async_copy(codes_hbm, codes, load_sem.at[1])]
+    for copy in loads:
+        copy.start()
     li, sc = lax.axis_index("lists"), lax.axis_index("score")
     mine = (sc // sizes[1], sc % sizes[1], li // sizes[3], li % sizes[3])
     rows = q_ref.shape[0]
@@ -129,7 +133,18 @@
     own_copies = [pltpu.make_async_copy(own(p), block(p, zero), own_sem.at[p]) for p in range(3)]
     for copy in own_copies:
         copy.start()
-    for part, back in sorted(itertools.product(range(3), places), key=cost):
+    nodes = sorted(itertools.product(range(3), places), key=cost)
+    held = codes.shape[0]
+    chunks = math.gcd(held, 8)
+    due = {3 + (len(nodes) - 3) * i // chunks: i for i in range(chunks)}
+    for turn, (part, back) in enumerate(nodes):
+        if turn == 3:
+            loads[0].wait()
+            widen(cent, wide)
+            loads[1].wait()
+        if turn in due:
+            blocks = held // chunks
+            rebuild(due[turn] * blocks, blocks, ids_ref, scales_ref, codes, wide, base, vecs_ref)
         order = orders[part]
         here = block(part, back)
         last = max([order.index(d) for d in range(4) if back[d]], default=-1)
@@ -161,27 +176,35 @@
         copy.wait()
 
 
-def spread(queries, asked, lists, score):
+def spread(queries, asked, ids, scales, centroids, codes, lists, score):
     rows, tokens, width = queries.shape
     vmem = pl.BlockSpec(memory_space=pltpu.VMEM)
+    smem = pl.BlockSpec(memory_space=pltpu.SMEM)
+    hbm = pl.BlockSpec(memory_space=pl.ANY)
     devices = lists * score
     return pl.pallas_call(
         functools.partial(spread_kernel, split_sizes(lists, score)),
         out_shape=[
             jax.ShapeDtypeStruct((score * rows, lists, tokens, width), queries.dtype),
             jax.ShapeDtypeStruct((devices,) + asked.shape, asked.dtype),
+            jax.ShapeDtypeStruct(codes.shape, jnp.bfloat16),
         ],
-        in_specs=[vmem] * 2,
-        out_specs=[vmem] * 2,
+        in_specs=[vmem, vmem, smem, vmem, hbm, hbm],
+        out_specs=[vmem] * 3,
         scratch_shapes=[
+            pltpu.VMEM(centroids.shape, centroids.dtype),
+            pltpu.VMEM(codes.shape, codes.dtype),
+            pltpu.VMEM(centroids.shape, jnp.float32),
+            pltpu.VMEM(codes.shape[1:], jnp.float32),
             pltpu.SemaphoreType.DMA((3, devices)),
             pltpu.SemaphoreType.DMA((3, devices)),
             pltpu.SemaphoreType.DMA((3,)),
+            pltpu.SemaphoreType.DMA((2,)),
         ],
         compiler_params=pltpu.CompilerParams(
-            collective_id=0, has_side_effects=True, vmem_limit_bytes=16 * 1024 * 1024
+            collective_id=0, has_side_effects=True, vmem_limit_bytes=32 * 1024 * 1024
         ),
-    )(queries, asked)
+    )(queries, asked, ids, scales, centroids, codes)
 
 
 def before(count):
@@ -198,7 +221,9 @@
     held = codes.shape[0]
 
     named_here = (owners[0] * held + slots[0]).reshape(-1, 128)
-    allq, asked = spread(queries, named_here, lists, score)
+    allq, asked, vecs = spread(
+        queries, named_here, centroid_ids, scales, centroids, codes, lists, score
+    )
     token_count, width = lists * queries.shape[1], queries.shape[2]
     allq = allq.reshape(score * query_rows, token_count, width)
     asked = asked.reshape(devices, query_rows, per_query)
@@ -216,10 +241,10 @@
     take = named[:, None, :] & (place[:, None, :] == jnp.arange(capacity, dtype=jnp.int32)[None, :, None])
     group = jnp.arange(devices, dtype=jnp.int32) % score
     query = group[:, None] * query_rows + jnp.arange(query_rows, dtype=jnp.int32)[None, :]
-    pickq = jnp.sum(jnp.where(take, query[:, None, :], 0), axis=2).reshape(-1)
-    picks = jnp.sum(jnp.where(take, slot[:, None, :], 0), axis=2).reshape(-1)
-
-    done = score_pairs(centroid_ids, lengths, pickq, picks, centroids, codes, scales, allq)
+    pick = query * held + slot
+    picks = jnp.sum(jnp.where(take, pick[:, None, :], 0), axis=2).reshape(-1)
+
+    done = score_pairs(lengths, picks, vecs, allq)
     done = done[:, :PAIRS].reshape(devices, capacity)
     full = jnp.sum(jnp.where(take, done[:, :, None], 0.0), axis=1)
     back = lax.all_to_all(full, AXES, split_axis=0, concat_axis=0, tiled=True)

time: 74.1 us -> 70.8 us (0.955)
  Pallas kernels: 48 us -> 46 us
  local copies, waits for them, and re-layouts: 10.1 us -> 9.35 us
    pallas_call x1, Pallas kernels: 25.4 us -> 15.9 us  [score_pairs(): pl.pallas_call(score_kernel, out_shape=jax.ShapeDtypeStruct((picks.shape[...]
    pallas_call x1, Pallas kernels: 22.6 us -> 30.1 us  [spread(): pl.pallas_call(functools.partial(spread_kernel, split_sizes(lists, score)...]
  transfers between devices with their start and end apart: 1 -> 1, of which waited for: 1 -> 1; matrix products, arithmetic and copies ran while one was open for 9% -> 10% of each run, Pallas kernels for 0% -> 0%
where the time goes in v3:
time: 70.8 us; the launch traced here: 70.4 us
  Pallas kernels  46 us (65%)
  local copies, waits for them, and re-layouts  9.35 us (13%)
  matrix products  6.93 us (10%)
  starting transfers between devices  4.52 us (6%)
  other arithmetic  2.52 us (4%)
  between operations  0.76 us (1%)
    pallas_call x1, Pallas kernels, spread(): pl.pallas_call(functools.partial(spread_kernel, split_sizes(lists, score)...  30.1 us
    pallas_call x1, Pallas kernels, score_pairs(): pl.pallas_call(score_kernel, out_shape=jax.ShapeDtypeStruct((picks.shape[...  15.9 us
    unnamed x21, local copies, waits for them, and re-layouts  8.7 us
    dot_general x1, matrix products, per_device(): lax.dot_general(mine.reshape(-1, width), centroids, (((1,), (1,)), ((), (...  6.73 us
    all_to_all x1, starting transfers between devices, per_device(): back = lax.all_to_all(full, AXES, split_axis=0, concat_axis=0, tiled=True)  4.52 us
  transfers between devices with their start and end apart: 1, of which 1 were waited for; matrix products, arithmetic and copies ran while one was open for 10% of the time, Pallas kernels for 0%

profile of v3, /device:TPU:0, one launch (start us, length us, event | category | flops | bytes accessed | tf_op | source)
XLA Modules:
  0.0 70.4 jit_solution(17291744291214571871)
XLA Ops:
  0.7 0.7 %multiply_add_fusion.1 = s32[1,32,8]{1,2,0:T(8,128)S(1)} fusion(s32[1,32,8]{1,2,0:T(8,128)} %param.15, s32[1,32,8]{1,2,0:T(8,128)} %param.14), kind=kLoop, calls=%fused_computation.23 | loop fusion | flops 512 | bytes 3072 | tf_op jit(solution)/shard_map/add | solution.py:223
  1.4 0.1 add.53.asked_ref
  1.5 1.6 %copy-done = bf16[8192,128]{1,0:T(8,128)(2,1)S(1)} copy-done((bf16[8192,128]{1,0:T(8,128)(2,1)S(1)}, bf16[8192,128]{1,0:T(8,128)(2,1)}, u32[]{:S(2)}) %copy-start) | copy-done | bytes 2097176
  3.1 1.2 %copy-done.4 = bf16[32,128,128]{2,1,0:T(8,128)(2,1)S(1)} copy-done((bf16[32,128,128]{2,1,0:T(8,128)(2,1)S(1)}, bf16[32,128,128]{2,1,0:T(8,128)(2,1)}, u32[]{:S(2)}) %copy-start.4) | copy-done | bytes 1048600
  4.4 0.8 %copy-done.5 = bf16[32,8,128]{2,1,0:T(8,128)(2,1)S(1)} copy-done((bf16[32,8,128]{2,1,0:T(8,128)(2,1)S(1)}, bf16[32,8,128]{2,1,0:T(8,128)(2,1)}, u32[]{:S(2)}) %copy-start.5) | copy-done | bytes 65560
  5.2 0.7 %copy-done.6 = s32[32,128]{1,0:T(8,128)S(1)} copy-done((s32[32,128]{1,0:T(8,128)S(1)}, s32[32,128]{1,0:T(8,128)}, u32[]{:S(2)}) %copy-start.6) | copy-done | bytes 16408
  5.9 0.7 %copy-done.7 = f32[32,128]{1,0:T(8,128)S(1)} copy-done((f32[32,128]{1,0:T(8,128)S(1)}, f32[32,128]{1,0:T(8,128)}, u32[]{:S(2)}) %copy-start.7) | copy-done | bytes 16408
  6.6 30.1 %shard_map.95 = (bf16[256,4,8,128]{3,2,1,0:T(8,128)(2,1)S(1)}, s32[32,2,128]{2,1,0:T(2,128)S(1)}, bf16[32,128,128]{2,1,0:T(8,128)(2,1)S(1)}) custom-call(bf16[32,8,128]{2,1,0:T(8,128)(2,1)S(1)} %copy-done.5, s32[2,128]{1,0:T(2,128)S(1)} %add.53.asked_ref, s32[32,128]{1,0:T(8,128)S(1)} %copy-done.6, f32[32,128]{1,0:T(8,128)S(1)} %copy-done.7, ...), custom_call_target="tpu_custom_call" | custom-call | tf_op jit(solution)/shard_map/pallas_call | solution.py:185
  36.7 1.3 %copy-done.2 = bf16[256,4,8,128]{3,2,1,0:T(8,128)(2,1)} copy-done((bf16[256,4,8,128]{3,2,1,0:T(8,128)(2,1)}, bf16[256,4,8,128]{3,2,1,0:T(8,128)(2,1)S(1)}, u32[]{:S(2)}) %copy-start.2) | copy-done | bytes 2097176
  38.1 0.1 copy.23
  38.2 0.1 fusion.10
  38.3 0.2 convolution_convert_fusion
  38.5 0.1 copy.24
  38.6 0.1 fusion.5
  38.8 0.6 select_reduce_fusion.1
  39.4 0.1 reshape.63.picks_ref
  39.5 1.6 %copy-done.3 = bf16[256,4,8,128]{3,2,1,0:T(8,128)(2,1)S(1)} copy-done((bf16[256,4,8,128]{3,2,1,0:T(8,128)(2,1)S(1)}, bf16[256,4,8,128]{3,2,1,0:T(8,128)(2,1)}, u32[]{:S(2)}) %copy-start.3) | copy-done | bytes 2097176
  41.1 15.9 %shard_map.96 = f32[32,128]{1,0:T(8,128)S(1)} custom-call(s32[32]{0:T(128)S(1)} %copy-done.8, s32[512]{0:T(512)S(1)} %reshape.63.picks_ref, bf16[32,128,128]{2,1,0:T(8,128)(2,1)S(1)} %get-tuple-element.6.vecs, bf16[256,32,128]{2,1,0:T(8,128)(2,1)S(1)} %bitcast.16), custom_call_target="tpu_custom_call" | custom-call | tf_op jit(solution)/shard_map/pallas_call | solution.py:71
  57.0 0.8 %select_reduce_fusion = f32[32,32]{1,0:T(8,128)} fusion(f32[32,16]{1,0:T(8,128)S(1)} %bitcast.17, s32[32,32]{1,0:T(8,128)S(1)} %convolution_convert_fusion, pred[32,32]{1,0:T(8,128)(4,1)S(1)} %copy.24), kind=kLoop, calls=%fused_computation.4 | loop fusion | flops 64512 | bytes 11264 | tf_op jit(solution)/shard_map/reduce_sum | solution.py:249
  57.8 4.5 %all-to-all-start = ((f32[32,1,32]{2,1,0:T(1,128)}), f32[32,1,32]{2,1,0:T(1,128)S(1)}, u32[]{:S(2)}, u32[]{:S(2)}) async-start(f32[32,1,32]{2,1,0:T(1,128)} %bitcast.4), calls=%async_computation | async-start | bytes 32768 | tf_op jit(solution)/shard_map/all_to_all | solution.py:250
  62.3 6.7 %convolution_reduce_fusion = f32[32,8192]{1,0:T(8,128)} fusion(bf16[8192,128]{1,0:T(8,128)(2,1)S(1)} %copy-done.1, bf16[256,32,128]{2,1,0:T(8,128)(2,1)} %bitcast.15, s32[]{:T(128)S(6)} %select_n.48), kind=kOutput, calls=%fused_computation | convolution fusion | flops 2155610112 | bytes 3407876 | tf_op jit(solution)/shard_map/dot_general | solution.py:232
  69.1 0.3 all-to-all-done
  69.5 0.2 select_reduce_fusion.2
  69.7 0.7 copy.28
  (19 shorter events, 0.3 us)
Async XLA Ops:
  0.6 38.9 %copy-start.8 = (s32[32]{0:T(128)S(1)}, s32[32]{0:T(128)}, u32[]{:S(2)}) copy-start(s32[32]{0:T(128)} %lens_ref.1) | copy-start | bytes 388
  1.5 1.6 %copy-start = (bf16[8192,128]{1,0:T(8,128)(2,1)S(1)}, bf16[8192,128]{1,0:T(8,128)(2,1)}, u32[]{:S(2)}) copy-start(bf16[8192,128]{1,0:T(8,128)(2,1)} %cent_hbm.1) | copy-start | bytes 6291460
  3.1 1.2 %copy-start.4 = (bf16[32,128,128]{2,1,0:T(8,128)(2,1)S(1)}, bf16[32,128,128]{2,1,0:T(8,128)(2,1)}, u32[]{:S(2)}) copy-start(bf16[32,128,128]{2,1,0:T(8,128)(2,1)} %codes_hbm.1) | copy-start | bytes 3145732
  4.4 0.8 %copy-start.5 = (bf16[32,8,128]{2,1,0:T(8,128)(2,1)S(1)}, bf16[32,8,128]{2,1,0:T(8,128)(2,1)}, u32[]{:S(2)}) copy-start(bf16[32,8,128]{2,1,0:T(8,128)(2,1)} %q_ref.1) | copy-start | bytes 196612
  5.2 0.7 %copy-start.6 = (s32[32,128]{1,0:T(8,128)S(1)}, s32[32,128]{1,0:T(8,128)}, u32[]{:S(2)}) copy-start(s32[32,128]{1,0:T(8,128)} %ids_ref.1) | copy-start | bytes 49156
  5.9 0.7 %copy-start.7 = (f32[32,128]{1,0:T(8,128)S(1)}, f32[32,128]{1,0:T(8,128)}, u32[]{:S(2)}) copy-start(f32[32,128]{1,0:T(8,128)} %scales_ref.1) | copy-start | bytes 49156
  36.7 1.4 %copy-start.2 = (bf16[256,4,8,128]{3,2,1,0:T(8,128)(2,1)}, bf16[256,4,8,128]{3,2,1,0:T(8,128)(2,1)S(1)}, u32[]{:S(2)}) copy-start(bf16[256,4,8,128]{3,2,1,0:T(8,128)(2,1)S(1)} %get-tuple-element.7) | copy-start | bytes 6291460
  38.1 24.2 %copy-start.1 = (bf16[8192,128]{1,0:T(8,128)(2,1)S(1)}, bf16[8192,128]{1,0:T(8,128)(2,1)}, u32[]{:S(2)}) copy-start(bf16[8192,128]{1,0:T(8,128)(2,1)} %cent_hbm.1) | copy-start | bytes 6291460
  39.5 1.6 %copy-start.3 = (bf16[256,4,8,128]{3,2,1,0:T(8,128)(2,1)S(1)}, bf16[256,4,8,128]{3,2,1,0:T(8,128)(2,1)}, u32[]{:S(2)}) copy-start(bf16[256,4,8,128]{3,2,1,0:T(8,128)(2,1)} %copy-done.2) | copy-start | bytes 6291460
  57.8 11.7 %all-to-all-start = ((f32[32,1,32]{2,1,0:T(1,128)}), f32[32,1,32]{2,1,0:T(1,128)S(1)}, u32[]{:S(2)}, u32[]{:S(2)}) async-start(f32[32,1,32]{2,1,0:T(1,128)} %bitcast.4), calls=%async_computation | async-start | bytes 32768 | tf_op jit(solution)/shard_map/all_to_all | solution.py:250
  62.3 6.7 %copy-start.9 = (s32[1,32,8]{1,2,0:T(8,128)S(1)}, s32[1,32,8]{1,2,0:T(8,128)}, u32[]{:S(2)}) copy-start(s32[1,32,8]{1,2,0:T(8,128)} %param.14) | copy-start | bytes 3076

commit v4 on v3

--- a/solution.py
+++ b/solution.py
@@ -9,7 +9,7 @@
 from jax.experimental.pallas import tpu as pltpu
 from jax.sharding import PartitionSpec as P
 
-PAIRS = 16
+PAIRS = 64
 ROWS = 16
 AXES = ("lists", "score")
 
@@ -87,10 +87,11 @@
 
 
 def spread_kernel(
-    sizes, q_ref, asked_ref, ids_ref, scales_ref, cent_hbm, codes_hbm, allq_ref, all_asked_ref, vecs_ref,
-    cent, codes, wide, base, send_sem, recv_sem, own_sem, load_sem,
+    sizes, q_ref, asked_ref, ids_hbm, scales_hbm, cent_hbm, codes_hbm, allq_ref, all_asked_ref, vecs_ref,
+    ids_ref, scales_ref, cent, codes, wide, base, send_sem, recv_sem, own_sem, load_sem,
 ):
-    loads = [pltpu.make_async_copy(cent_hbm, cent, load_sem.at[0]), pltpu.make_async_copy(codes_hbm, codes, load_sem.at[1])]
+    pairs = ((cent_hbm, cent), (codes_hbm, codes), (ids_hbm, ids_ref), (scales_hbm, scales_ref))
+    loads = [pltpu.make_async_copy(src, dst, load_sem.at[i]) for i, (src, dst) in enumerate(pairs)]
     for copy in loads:
         copy.start()
     li, sc = lax.axis_index("lists"), lax.axis_index("score")
@@ -141,7 +142,8 @@
         if turn == 3:
             loads[0].wait()
             widen(cent, wide)
-            loads[1].wait()
+            for copy in loads[1:]:
+                copy.wait()
         if turn in due:
             blocks = held // chunks
             rebuild(due[turn] * blocks, blocks, ids_ref, scales_ref, codes, wide, base, vecs_ref)
@@ -179,8 +181,7 @@
 def spread(queries, asked, ids, scales, centroids, codes, lists, score):
     rows, tokens, width = queries.shape
     vmem = pl.BlockSpec(memory_space=pltpu.VMEM)
-    smem = pl.BlockSpec(memory_space=pltpu.SMEM)
-    hbm = pl.BlockSpec(memory_space=pl.ANY)
+    hbm = pl.BlockSpec(memory_space=pltpu.MemorySpace.HBM)
     devices = lists * score
     return pl.pallas_call(
         functools.partial(spread_kernel, split_sizes(lists, score)),
@@ -189,9 +190,11 @@
             jax.ShapeDtypeStruct((devices,) + asked.shape, asked.dtype),
             jax.ShapeDtypeStruct(codes.shape, jnp.bfloat16),
         ],
-        in_specs=[vmem, vmem, smem, vmem, hbm, hbm],
+        in_specs=[hbm, vmem, hbm, hbm, hbm, hbm],
         out_specs=[vmem] * 3,
         scratch_shapes=[
+            pltpu.SMEM(ids.shape, ids.dtype),
+            pltpu.VMEM(scales.shape, scales.dtype),
             pltpu.VMEM(centroids.shape, centroids.dtype),
             pltpu.VMEM(codes.shape, codes.dtype),
             pltpu.VMEM(centroids.shape, jnp.float32),
@@ -199,10 +202,10 @@
             pltpu.SemaphoreType.DMA((3, devices)),
             pltpu.SemaphoreType.DMA((3, devices)),
             pltpu.SemaphoreType.DMA((3,)),
-            pltpu.SemaphoreType.DMA((2,)),
+            pltpu.SemaphoreType.DMA((4,)),
         ],
         compiler_params=pltpu.CompilerParams(
-            collective_id=0, has_side_effects=True, vmem_limit_bytes=32 * 1024 * 1024
+            collective_id=0, has_side_effects=True, vmem_limit_bytes=58 * 1024 * 1024
         ),
     )(queries, asked, ids, scales, centroids, codes)
 

time: 70.8 us -> 63.5 us (0.90)
  local copies, waits for them, and re-layouts: 9.35 us -> 5.54 us
  Pallas kernels: 46 us -> 42.6 us
    unnamed x21 -> x11, local copies, waits for them, and re-layouts: 8.7 us -> 3.5 us
    pallas_call x1, Pallas kernels: 15.9 us -> 10.9 us  [score_pairs(): pl.pallas_call(score_kernel, out_shape=jax.ShapeDtypeStruct((picks.shape[...]
    pallas_call x1, Pallas kernels: 30.1 us -> 31.6 us  [spread(): pl.pallas_call(functools.partial(spread_kernel, split_sizes(lists, score)...]
    pallas_call x1, local copies, waits for them, and re-layouts: 0.1 us -> 0.85 us  [spread(): pl.pallas_call(functools.partial(spread_kernel, split_sizes(lists, score)...]
  transfers between devices with their start and end apart: 1 -> 1, of which waited for: 1 -> 1; matrix products, arithmetic and copies ran while one was open for 10% -> 11% of each run, Pallas kernels for 0% -> 0%
where the time goes in v4:
time: 63.5 us; the launch traced here: 63.1 us
  Pallas kernels  42.6 us (67%)
  matrix products  6.93 us (11%)
  local copies, waits for them, and re-layouts  5.54 us (9%)
  starting transfers between devices  4.54 us (7%)
  other arithmetic  2.52 us (4%)
  between operations  0.74 us (1%)
    pallas_call x1, Pallas kernels, spread(): pl.pallas_call(functools.partial(spread_kernel, split_sizes(lists, score)...  31.6 us
    pallas_call x1, Pallas kernels, score_pairs(): pl.pallas_call(score_kernel, out_shape=jax.ShapeDtypeStruct((picks.shape[...  10.9 us
    dot_general x1, matrix products, per_device(): lax.dot_general(mine.reshape(-1, width), centroids, (((1,), (1,)), ((), (...  6.73 us
    all_to_all x1, starting transfers between devices, per_device(): back = lax.all_to_all(full, AXES, split_axis=0, concat_axis=0, tiled=True)  4.54 us
    unnamed x11, local copies, waits for them, and re-layouts  3.5 us
  transfers between devices with their start and end apart: 1, of which 1 were waited for; matrix products, arithmetic and copies ran while one was open for 11% of the time, Pallas kernels for 0%

profile of v4, /device:TPU:0, one launch (start us, length us, event | category | flops | bytes accessed | tf_op | source)
XLA Modules:
  0.0 63.1 jit_solution(16067022327026498617)
XLA Ops:
  0.7 0.7 %multiply_add_fusion.1 = s32[1,32,8]{1,2,0:T(8,128)S(1)} fusion(s32[1,32,8]{1,2,0:T(8,128)} %param.15, s32[1,32,8]{1,2,0:T(8,128)} %param.14), kind=kLoop, calls=%fused_computation.23 | loop fusion | flops 512 | bytes 3072 | tf_op jit(solution)/shard_map/add | solution.py:226
  1.4 0.1 copy.22
  1.4 0.7 %add.53.asked_ref = s32[2,128]{1,0:T(2,128)} reshape(s32[1,32,8]{2,1,0:T(8,128)S(1)} %copy.22) | data formatting | bytes 2048 | tf_op jit(solution)/shard_map/add | solution.py:226
  2.1 31.6 %shard_map.95 = (bf16[256,4,8,128]{3,2,1,0:T(8,128)(2,1)}, s32[32,2,128]{2,1,0:T(2,128)}, bf16[32,128,128]{2,1,0:T(8,128)(2,1)}) custom-call(bf16[32,8,128]{2,1,0:T(8,128)(2,1)} %q_ref.1, s32[2,128]{1,0:T(2,128)} %add.53.asked_ref, s32[32,128]{1,0:T(8,128)} %ids_hbm.1, f32[32,128]{1,0:T(8,128)} %scales_hbm.1, bf16[8192,128]{1,0:T(8,128)(2,1)} %cent_hbm.1, ...), custom_call_target="tpu_custom_call" | custom-call | tf_op jit(solution)/shard_map/pallas_call | solution.py:186
  33.7 0.9 %copy.23 = s32[32,2,128]{0,2,1:T(8,128)S(1)} copy(s32[32,2,128]{2,1,0:T(2,128)} %get-tuple-element.5) | data formatting | bytes 65536 | tf_op jit(solution)/shard_map/pallas_call | solution.py:186
  34.6 0.1 fusion.10
  34.7 0.2 convolution_convert_fusion
  34.9 0.1 copy.24
  35.0 0.1 fusion.5
  35.1 0.1 copy.25
  35.2 0.6 select_reduce_fusion.1
  35.8 0.1 reshape.63.picks_ref
  35.9 1.6 %copy-done = bf16[256,4,8,128]{3,2,1,0:T(8,128)(2,1)S(1)} copy-done((bf16[256,4,8,128]{3,2,1,0:T(8,128)(2,1)S(1)}, bf16[256,4,8,128]{3,2,1,0:T(8,128)(2,1)}, u32[]{:S(2)}) %copy-start) | copy-done | bytes 2097176
  37.5 1.2 %copy-done.1 = bf16[32,128,128]{2,1,0:T(8,128)(2,1)S(1)} copy-done((bf16[32,128,128]{2,1,0:T(8,128)(2,1)S(1)}, bf16[32,128,128]{2,1,0:T(8,128)(2,1)}, u32[]{:S(2)}) %copy-start.1) | copy-done | bytes 1048600
  38.7 10.9 %shard_map.96 = f32[8,128]{1,0:T(8,128)S(1)} custom-call(s32[32]{0:T(128)S(1)} %copy-done.2, s32[512]{0:T(512)S(1)} %reshape.63.picks_ref, bf16[32,128,128]{2,1,0:T(8,128)(2,1)S(1)} %copy-done.1, bf16[256,32,128]{2,1,0:T(8,128)(2,1)S(1)} %bitcast.16), custom_call_target="tpu_custom_call" | custom-call | tf_op jit(solution)/shard_map/pallas_call | solution.py:71
  49.7 0.1 broadcast_in_dim.55
  49.8 0.8 %select_reduce_fusion = f32[32,32]{1,0:T(8,128)} fusion(f32[32,16]{1,0:T(8,128)S(1)} %broadcast_in_dim.55, s32[32,32]{1,0:T(8,128)S(1)} %convolution_convert_fusion, pred[32,32]{1,0:T(8,128)(4,1)S(1)} %copy.24), kind=kLoop, calls=%fused_computation.4 | loop fusion | flops 64512 | bytes 11264 | tf_op jit(solution)/shard_map/reduce_sum | solution.py:252
  50.5 4.5 %all-to-all-start = ((f32[32,1,32]{2,1,0:T(1,128)}), f32[32,1,32]{2,1,0:T(1,128)S(1)}, u32[]{:S(2)}, u32[]{:S(2)}) async-start(f32[32,1,32]{2,1,0:T(1,128)} %bitcast.4), calls=%async_computation | async-start | bytes 32768 | tf_op jit(solution)/shard_map/all_to_all | solution.py:253
  55.1 6.7 %convolution_reduce_fusion = f32[32,8192]{1,0:T(8,128)} fusion(bf16[8192,128]{1,0:T(8,128)(2,1)S(1)} %copy-done.3, bf16[256,32,128]{2,1,0:T(8,128)(2,1)} %bitcast.15, s32[]{:T(128)S(6)} %select_n.48), kind=kOutput, calls=%fused_computation | convolution fusion | flops 2155610112 | bytes 3407876 | tf_op jit(solution)/shard_map/dot_general | solution.py:235
  61.8 0.1 copy.21
  61.9 0.3 all-to-all-done
  62.2 0.1 copy.27
  62.3 0.2 select_reduce_fusion.2
  62.5 0.7 %copy.28 = f32[1,32,8]{1,2,0:T(8,128)} copy(f32[1,32,8]{2,1,0:T(8,128)S(1)} %bitcast.20) | data formatting | bytes 2048
  (10 shorter events, 0.0 us)
Async XLA Ops:
  0.6 35.3 %copy-start.2 = (s32[32]{0:T(128)S(1)}, s32[32]{0:T(128)}, u32[]{:S(2)}) copy-start(s32[32]{0:T(128)} %lens_ref.1) | copy-start | bytes 388
  2.1 53.0 %copy-start.3 = (bf16[8192,128]{1,0:T(8,128)(2,1)S(1)}, bf16[8192,128]{1,0:T(8,128)(2,1)}, u32[]{:S(2)}) copy-start(bf16[8192,128]{1,0:T(8,128)(2,1)} %cent_hbm.1) | copy-start | bytes 6291460
  35.9 1.6 %copy-start = (bf16[256,4,8,128]{3,2,1,0:T(8,128)(2,1)S(1)}, bf16[256,4,8,128]{3,2,1,0:T(8,128)(2,1)}, u32[]{:S(2)}) copy-start(bf16[256,4,8,128]{3,2,1,0:T(8,128)(2,1)} %get-tuple-element.7) | copy-start | bytes 6291460
  37.5 1.2 %copy-start.1 = (bf16[32,128,128]{2,1,0:T(8,128)(2,1)S(1)}, bf16[32,128,128]{2,1,0:T(8,128)(2,1)}, u32[]{:S(2)}) copy-start(bf16[32,128,128]{2,1,0:T(8,128)(2,1)} %get-tuple-element.6.vecs) | copy-start | bytes 3145732
  50.5 11.7 %all-to-all-start = ((f32[32,1,32]{2,1,0:T(1,128)}), f32[32,1,32]{2,1,0:T(1,128)S(1)}, u32[]{:S(2)}, u32[]{:S(2)}) async-start(f32[32,1,32]{2,1,0:T(1,128)} %bitcast.4), calls=%async_computation | async-start | bytes 32768 | tf_op jit(solution)/shard_map/all_to_all | solution.py:253
  55.1 6.7 %copy-start.4 = (s32[1,32,8]{1,2,0:T(8,128)S(1)}, s32[1,32,8]{1,2,0:T(8,128)}, u32[]{:S(2)}) copy-start(s32[1,32,8]{1,2,0:T(8,128)} %param.14) | copy-start | bytes 3076
